TPU v7x, 32 devices: a whole 2x2x4 slice. The times are simulated.
32 devices in a mesh: slab: 8 (over y, x, core), lat: 4 (over z).
Axes of the slice: x: 2, y: 2, z: 4, core: 2. Of those that a mesh axis runs over, the one named last changes fastest.
Arguments:
- tokens: bfloat16 [16, 16, 16, 1024], P(None, 'lat', 'slab'), may hold values from -6 to 6
- conv_first: float32 [27, 1024], replicated, may hold values from -1.25 to 1.25
- conv_second: float32 [27, 1024], replicated, may hold values from -1.25 to 1.25
- kv_weight: bfloat16 [2, 1024, 1024], P(None, None, 'lat'), may hold values from -0.1875 to 0.1875
- queries: bfloat16 [512, 1024], replicated, may hold values from -70 to 70
Outputs:
- decoded: bfloat16 [16, 16, 16, 1024], P(None, 'lat', 'slab')
All inputs are finite; a program needn't handle non-finite values.
Results may differ from a plain program's by a relative error of at most 0.012.
The roundings to bfloat16 on the way count: a program that leaves them out, or rounds other values in their place, can miss the bound.
Values may be sent and summed in bfloat16 or wider, within the bound.
No kernel may reach another device: no remote copies, remote signals or barrier semaphores. Data moves between devices by JAX's collectives and lax.ppermute only.
A program may use at most 64 MiB of HBM per device.

v0:
```python
import jax
import jax.numpy as jnp
from jax import lax
from jax.sharding import PartitionSpec as P


def with_halo(block, sides, width):
    for axis, dim in sides:
        count = lax.axis_size(axis)
        forward = [(i, i + 1) for i in range(count - 1)]
        backward = [(target, source) for source, target in forward]
        low = lax.ppermute(
            lax.slice_in_dim(block, block.shape[dim] - width, None, axis=dim), axis, forward
        )
        high = lax.ppermute(lax.slice_in_dim(block, 0, width, axis=dim), axis, backward)
        block = jnp.concatenate([low, block, high], axis=dim)
    return block


def conv_valid(padded, weights):
    size_x = padded.shape[0] - 2
    size_y = padded.shape[1] - 2
    size_z = padded.shape[2] - 2
    accum_sum = jnp.zeros((size_x, size_y, size_z, padded.shape[3]), jnp.float32)
    for tap_index in range(27):
        shift_x = tap_index // 9
        shift_y = tap_index // 3 % 3
        shift_z = tap_index % 3
        window = padded[
            shift_x : shift_x + size_x, shift_y : shift_y + size_y, shift_z : shift_z + size_z
        ]
        accum_sum = accum_sum + weights[tap_index] * window
    return accum_sum


def extend_first(field):
    return jnp.pad(field.astype(jnp.float32), ((1, 1), (0, 0), (0, 0), (0, 0)))


def local(tokens, conv_first, conv_second, kv_weight, queries):
    width = tokens.shape[3]
    source = tokens.astype(jnp.float32)
    padded_tokens = with_halo(tokens, (("slab", 2), ("lat", 1)), 1)
    inner_layer = jax.nn.gelu(conv_valid(extend_first(padded_tokens), conv_first)).astype(
        jnp.bfloat16
    )
    beside_all = with_halo(inner_layer, (("slab", 2), ("lat", 1)), 1)
    mixed = jax.nn.gelu(conv_valid(extend_first(beside_all), conv_second))
    hidden = (source + mixed).astype(jnp.bfloat16)
    token_rows = hidden.reshape(-1, width)
    product = jnp.einsum(
        "td,kdw->ktw",
        token_rows,
        lax.all_gather(kv_weight, "lat", axis=2, tiled=True),
        preferred_element_type=jnp.float32,
    )
    projected = product.astype(jnp.bfloat16)
    key_rows = projected[0]
    value_rows = projected[1]
    score_scale = 1.0 / width**0.5
    scores = (
        jnp.einsum("ld,td->lt", queries, key_rows, preferred_element_type=jnp.float32) * score_scale
    )
    local_max = jnp.max(scores, axis=1)
    maximum = lax.pmax(local_max, ("slab", "lat"))
    exponent = jnp.exp(scores - maximum[:, None])
    weights_bf = exponent.astype(jnp.bfloat16)
    denominator = jnp.sum(exponent, axis=1)
    numerator = jnp.dot(weights_bf, value_rows, preferred_element_type=jnp.float32)
    numer_total, denom_total = lax.psum((numerator, denominator), ("slab", "lat"))
    latents = (numer_total / denom_total[:, None]).astype(jnp.bfloat16)
    back = (
        jnp.einsum("td,ld->tl", token_rows, latents, preferred_element_type=jnp.float32)
        * score_scale
    )
    probs = jax.nn.softmax(back, axis=1).astype(jnp.bfloat16)
    result = token_rows.astype(jnp.float32) + jnp.dot(
        probs, latents, preferred_element_type=jnp.float32
    )
    return result.astype(jnp.bfloat16).reshape(hidden.shape)


def solution(mesh):
    placed = (P(None, "lat", "slab", None), P(), P(), P(None, None, "lat"), P())
    return jax.shard_map(
        local, mesh=mesh, in_specs=placed, out_specs=P(None, "lat", "slab", None), check_vma=False
    )
```

profile of v0, /device:TPU:0, one launch (start us, length us, event | category | flops | bytes accessed | tf_op | source)
XLA Modules:
  0.0 288.1 jit_solution(4803963372032662820)
XLA Ops:
  7.3 1.6 fusion.90
  8.9 2.4 collective-permute-start
  11.4 1.3 collective-permute-start.1
  12.7 4.1 %collective-permute-done.1 = bf16[16,4,1,1024]{3,2,1,0:T(2,128)(2,1)S(1)} collective-permute-done((bf16[16,4,1,1024]{3,2,1,0:T(2,128)(2,1)S(1)}, bf16[16,4,1,1024]{3,2,1,0:T(2,128)(2,1)S(1)}, u32[]{:S(2)}, u32[]{:S(2)}) %collective-permute-start.1) | collective-permute-done | bytes 131104 | tf_op jit(solution)/shard_map/ppermute | solution.py:15
  17.3 3.5 %collective-permute-start.2 = (bf16[16,1,4,1024]{3,2,1,0:T(4,128)(2,1)S(1)}, bf16[16,1,4,1024]{3,2,1,0:T(4,128)(2,1)S(1)}, u32[]{:S(2)}, u32[]{:S(2)}) collective-permute-start(bf16[16,1,4,1024]{3,2,1,0:T(4,128)(2,1)S(1)} %get-tuple-element.7), channel_id=1, source_target_pairs={{0,1},{1,2},{2,3},{4,5},{5,6},{6,7},{8,9},{9,10},{10,11},{12,13},{... | collective-permute-start | bytes 393224 | tf_op jit(solution)/shard_map/ppermute | solution.py:12
  20.8 1.3 collective-permute-start.3
  22.2 4.1 %collective-permute-done.2 = bf16[16,1,4,1024]{3,2,1,0:T(4,128)(2,1)S(1)} collective-permute-done((bf16[16,1,4,1024]{3,2,1,0:T(4,128)(2,1)S(1)}, bf16[16,1,4,1024]{3,2,1,0:T(4,128)(2,1)S(1)}, u32[]{:S(2)}, u32[]{:S(2)}) %collective-permute-start.2) | collective-permute-done | bytes 131104 | tf_op jit(solution)/shard_map/ppermute | solution.py:12
  26.2 5.3 %collective-permute-done.3 = bf16[16,1,4,1024]{3,2,1,0:T(4,128)(2,1)S(1)} collective-permute-done((bf16[16,1,4,1024]{3,2,1,0:T(4,128)(2,1)S(1)}, bf16[16,1,4,1024]{3,2,1,0:T(4,128)(2,1)S(1)}, u32[]{:S(2)}, u32[]{:S(2)}) %collective-permute-start.3) | collective-permute-done | bytes 131104 | tf_op jit(solution)/shard_map/ppermute | solution.py:15
  32.5 6.8 %fusion.79 = bf16[16,4,2,1024]{3,2,1,0:T(2,128)(2,1)S(1)} fusion(f32[16,6,4,1024]{3,2,1,0:T(4,128)S(1)} %maximum_convert_fusion, f32[1024]{0:T(1024)S(1)} %bitcast.122, f32[1024]{0:T(1024)S(1)} %bitcast.123, f32[1024]{0:T(1024)S(1)} %bitcast.98, f32[1024]{0:T(1024)S(1)} %bitcast.99, f32[1024]{0:T(1024)S(1)} %bitcast.100, f32[1024]{0:T(1024)S(1)} %bitcast.101, ...), kind=kLoop, calls=%fused_computation.126 | loop fusion | flops 8126464 | bytes 6664192 | tf_op jit(solution)/shard_map/convert_element_type | solution.py:44
  39.9 6.2 %collective-permute-start.4 = (bf16[16,4,1,1024]{3,2,1,0:T(2,128)(2,1)S(1)}, bf16[16,4,1,1024]{3,2,1,0:T(2,128)(2,1)S(1)}, u32[]{:S(2)}, u32[]{:S(2)}) collective-permute-start(bf16[16,4,1,1024]{3,2,1,0:T(2,128)(2,1)S(1)} %get-tuple-element.9), channel_id=1, source_target_pairs={{0,4},{4,8},{8,12},{12,16},{16,20},{20,24},{24,28},{1,5},{5,9},{9,... | collective-permute-start | bytes 393224 | tf_op jit(solution)/shard_map/ppermute | solution.py:12
  46.1 1.3 collective-permute-start.5
  47.5 2.7 collective-permute-done.5
  50.7 8.4 %collective-permute-start.6 = (bf16[16,1,4,1024]{3,2,1,0:T(4,128)(2,1)S(1)}, bf16[16,1,4,1024]{3,2,1,0:T(4,128)(2,1)S(1)}, u32[]{:S(2)}, u32[]{:S(2)}) collective-permute-start(bf16[16,1,4,1024]{3,2,1,0:T(4,128)(2,1)S(1)} %get-tuple-element.5), channel_id=1, source_target_pairs={{0,1},{1,2},{2,3},{4,5},{5,6},{6,7},{8,9},{9,10},{10,11},{12,13},{... | collective-permute-start | bytes 393224 | tf_op jit(solution)/shard_map/ppermute | solution.py:12
  59.1 1.3 collective-permute-start.7
  60.4 4.1 %collective-permute-done.6 = bf16[16,1,4,1024]{3,2,1,0:T(4,128)(2,1)S(1)} collective-permute-done((bf16[16,1,4,1024]{3,2,1,0:T(4,128)(2,1)S(1)}, bf16[16,1,4,1024]{3,2,1,0:T(4,128)(2,1)S(1)}, u32[]{:S(2)}, u32[]{:S(2)}) %collective-permute-start.6) | collective-permute-done | bytes 131104 | tf_op jit(solution)/shard_map/ppermute | solution.py:12
  64.5 12.2 %collective-permute-done.7 = bf16[16,1,4,1024]{3,2,1,0:T(4,128)(2,1)S(1)} collective-permute-done((bf16[16,1,4,1024]{3,2,1,0:T(4,128)(2,1)S(1)}, bf16[16,1,4,1024]{3,2,1,0:T(4,128)(2,1)S(1)}, u32[]{:S(2)}, u32[]{:S(2)}) %collective-permute-start.7) | collective-permute-done | bytes 131104 | tf_op jit(solution)/shard_map/ppermute | solution.py:15
  77.7 7.0 %fusion.80 = bf16[16,4,2,1024]{3,2,1,0:T(2,128)(2,1)S(1)} fusion(f32[16,6,4,1024]{3,2,1,0:T(4,128)S(1)} %maximum_convert_fusion.1, bf16[16,4,2,1024]{3,2,1,0:T(2,128)(2,1)S(1)} %copy-done.1, f32[1024]{0:T(1024)S(1)} %bitcast.95, f32[1024]{0:T(1024)S(1)} %bitcast.96, f32[1024]{0:T(1024)S(1)} %bitcast.71, f32[1024]{0:T(1024)S(1)} %bitcast.72, ...), kind=kLoop, calls=%fused_computation.127 | loop fusion | flops 8388608 | bytes 6926336 | tf_op jit(solution)/shard_map/convert_element_type | solution.py:49
  84.8 13.0 %all-gather.2.cloned.1.call-done = bf16[2,1024,1024]{2,1,0:T(8,128)(2,1)} async-done(((bf16[2,1024,256]{2,1,0:T(8,128)(2,1)}), bf16[2,1024,1024]{2,1,0:T(8,128)(2,1)}) %all-gather.2.cloned.1.call-update) | async-done | bytes 4194320 | tf_op jit(solution)/shard_map/all_gather | solution.py:54
  97.8 2.9 %fusion = bf16[2,128,1024]{2,1,0:T(8,128)(2,1)S(1)} fusion(bf16[128,1024,1]{1,0,2:T(8,128)(2,1)S(1)} %reshape.66, bf16[2,1024,1024]{2,1,0:T(8,128)(2,1)} %all-gather.2.cloned.1.call-done), kind=kOutput, calls=%fused_computation.3 | convolution fusion | flops 537133056 | bytes 4980736 | tf_op jit(solution)/shard_map/td,kdw->ktw/dot_general | solution.py:51
  101.2 39.5 %pmax.7 = f32[512]{0:T(512)S(1)} all-reduce(f32[512]{0:T(512)S(1)} %get-tuple-element.67), channel_id=1, replica_groups=mesh['slab'=8,'lat'=4] {'slab','lat'}, use_global_device_ids=true, to_apply=%region_1.2 | all-reduce | flops 512 | bytes 4096 | tf_op jit(solution)/shard_map/pmax | solution.py:65
  140.7 1.8 fusion.81
  142.6 40.4 %psum.15 = f32[512]{0:T(512)S(1)} all-reduce(f32[512]{0:T(512)S(1)} %fusion.82), channel_id=1, replica_groups=mesh['slab'=8,'lat'=4] {'slab','lat'}, use_global_device_ids=true, to_apply=%region_4.5 | all-reduce | flops 512 | bytes 4096 | tf_op jit(solution)/shard_map/psum | solution.py:70
  183.1 94.3 %all-reduce.4.cloned.1.call-done = f32[512,1024]{1,0:T(8,128)} async-done(((f32[512,1024]{1,0:T(8,128)}), f32[512,1024]{1,0:T(8,128)}) %all-reduce.4.cloned.1.call-update) | async-done | bytes 2097168 | tf_op jit(solution)/shard_map/psum | solution.py:70
  277.4 1.9 divide_convert_fusion
  (31 shorter events, 7.0 us)
Async XLA Ops:
  6.5 94.1 %copy-start = (bf16[512,1024]{1,0:T(8,128)(2,1)S(1)}, bf16[512,1024]{1,0:T(8,128)(2,1)}, u32[]{:S(2)}) copy-start(bf16[512,1024]{1,0:T(8,128)(2,1)} %param.9) | copy-start | bytes 3145732
  6.5 10.3 %copy-start.1 = (bf16[16,4,2,1024]{3,2,1,0:T(2,128)(2,1)S(1)}, bf16[16,4,2,1024]{3,2,1,0:T(2,128)(2,1)}, u32[]{:S(2)}) copy-start(bf16[16,4,2,1024]{3,2,1,0:T(2,128)(2,1)} %param.5) | copy-start | bytes 786436
  6.5 6.1 %copy-start.2 = (f32[27,1024]{1,0:T(8,128)S(1)}, f32[27,1024]{1,0:T(8,128)}, u32[]{:S(2)}) copy-start(f32[27,1024]{1,0:T(8,128)} %param.6) | copy-start | bytes 331780
  6.5 91.2 %all-gather.2.cloned.1.call-start = ((), (), s32[]{:S(2)}) async-start(), calls=%async_computation | async-start | bytes 5242880 | tf_op jit(solution)/shard_map/all_gather | solution.py:54
  7.3 270.1 %all-reduce.4.cloned.1.call-start = ((), (), s32[]{:S(2)}) async-start(), calls=%async_computation.1 | async-start | bytes 4194304 | tf_op jit(solution)/shard_map/psum | solution.py:70
  8.9 3.8 %collective-permute-start = (bf16[16,4,1,1024]{3,2,1,0:T(2,128)(2,1)S(1)}, bf16[16,4,1,1024]{3,2,1,0:T(2,128)(2,1)S(1)}, u32[]{:S(2)}, u32[]{:S(2)}) collective-permute-start(bf16[16,4,1,1024]{3,2,1,0:T(2,128)(2,1)S(1)} %get-tuple-element.11), channel_id=1, source_target_pairs={{0,4},{4,8},{8,12},{12,16},{16,20},{20,24},{24,28},{1,5},{5,9},{9,... | collective-permute-start | bytes 393224 | tf_op jit(solution)/shard_map/ppermute | solution.py:12
  11.4 5.5 %collective-permute-start.1 = (bf16[16,4,1,1024]{3,2,1,0:T(2,128)(2,1)S(1)}, bf16[16,4,1,1024]{3,2,1,0:T(2,128)(2,1)S(1)}, u32[]{:S(2)}, u32[]{:S(2)}) collective-permute-start(bf16[16,4,1,1024]{3,2,1,0:T(2,128)(2,1)S(1)} %get-tuple-element.12), channel_id=1, source_target_pairs={{4,0},{8,4},{12,8},{16,12},{20,16},{24,20},{28,24},{5,1},{9,5},{13... | collective-permute-start | bytes 393224 | tf_op jit(solution)/shard_map/ppermute | solution.py:15
  17.3 8.9 %collective-permute-start.2 = (bf16[16,1,4,1024]{3,2,1,0:T(4,128)(2,1)S(1)}, bf16[16,1,4,1024]{3,2,1,0:T(4,128)(2,1)S(1)}, u32[]{:S(2)}, u32[]{:S(2)}) collective-permute-start(bf16[16,1,4,1024]{3,2,1,0:T(4,128)(2,1)S(1)} %get-tuple-element.7), channel_id=1, source_target_pairs={{0,1},{1,2},{2,3},{4,5},{5,6},{6,7},{8,9},{9,10},{10,11},{12,13},{... | collective-permute-start | bytes 393224 | tf_op jit(solution)/shard_map/ppermute | solution.py:12
  20.8 10.7 %collective-permute-start.3 = (bf16[16,1,4,1024]{3,2,1,0:T(4,128)(2,1)S(1)}, bf16[16,1,4,1024]{3,2,1,0:T(4,128)(2,1)S(1)}, u32[]{:S(2)}, u32[]{:S(2)}) collective-permute-start(bf16[16,1,4,1024]{3,2,1,0:T(4,128)(2,1)S(1)} %get-tuple-element.8), channel_id=1, source_target_pairs={{1,0},{2,1},{3,2},{5,4},{6,5},{7,6},{9,8},{10,9},{11,10},{13,12},{... | collective-permute-start | bytes 393224 | tf_op jit(solution)/shard_map/ppermute | solution.py:15
  32.5 14.9 %copy-start.3 = (f32[27,1024]{1,0:T(8,128)S(1)}, f32[27,1024]{1,0:T(8,128)}, u32[]{:S(2)}) copy-start(f32[27,1024]{1,0:T(8,128)} %param.7) | copy-start | bytes 331780
  39.9 7.6 %collective-permute-start.4 = (bf16[16,4,1,1024]{3,2,1,0:T(2,128)(2,1)S(1)}, bf16[16,4,1,1024]{3,2,1,0:T(2,128)(2,1)S(1)}, u32[]{:S(2)}, u32[]{:S(2)}) collective-permute-start(bf16[16,4,1,1024]{3,2,1,0:T(2,128)(2,1)S(1)} %get-tuple-element.9), channel_id=1, source_target_pairs={{0,4},{4,8},{8,12},{12,16},{16,20},{20,24},{24,28},{1,5},{5,9},{9,... | collective-permute-start | bytes 393224 | tf_op jit(solution)/shard_map/ppermute | solution.py:12
  46.1 4.1 %collective-permute-start.5 = (bf16[16,4,1,1024]{3,2,1,0:T(2,128)(2,1)S(1)}, bf16[16,4,1,1024]{3,2,1,0:T(2,128)(2,1)S(1)}, u32[]{:S(2)}, u32[]{:S(2)}) collective-permute-start(bf16[16,4,1,1024]{3,2,1,0:T(2,128)(2,1)S(1)} %get-tuple-element.10), channel_id=1, source_target_pairs={{4,0},{8,4},{12,8},{16,12},{20,16},{24,20},{28,24},{5,1},{9,5},{13... | collective-permute-start | bytes 393224 | tf_op jit(solution)/shard_map/ppermute | solution.py:15
  50.7 13.8 %collective-permute-start.6 = (bf16[16,1,4,1024]{3,2,1,0:T(4,128)(2,1)S(1)}, bf16[16,1,4,1024]{3,2,1,0:T(4,128)(2,1)S(1)}, u32[]{:S(2)}, u32[]{:S(2)}) collective-permute-start(bf16[16,1,4,1024]{3,2,1,0:T(4,128)(2,1)S(1)} %get-tuple-element.5), channel_id=1, source_target_pairs={{0,1},{1,2},{2,3},{4,5},{5,6},{6,7},{8,9},{9,10},{10,11},{12,13},{... | collective-permute-start | bytes 393224 | tf_op jit(solution)/shard_map/ppermute | solution.py:12
  59.1 17.6 %collective-permute-start.7 = (bf16[16,1,4,1024]{3,2,1,0:T(4,128)(2,1)S(1)}, bf16[16,1,4,1024]{3,2,1,0:T(4,128)(2,1)S(1)}, u32[]{:S(2)}, u32[]{:S(2)}) collective-permute-start(bf16[16,1,4,1024]{3,2,1,0:T(4,128)(2,1)S(1)} %get-tuple-element.6), channel_id=1, source_target_pairs={{1,0},{2,1},{3,2},{5,4},{6,5},{7,6},{9,8},{10,9},{11,10},{13,12},{... | collective-permute-start | bytes 393224 | tf_op jit(solution)/shard_map/ppermute | solution.py:15
Sparse Core Ops, SparseCore 0:
  8.9 88.8 all-gather.1
  142.6 134.7 all-reduce.3
where the time goes:
time: 289 us; the launch traced here: 288 us
  waiting for transfers between devices  141 us (49%)
  blocking collectives  79.9 us (28%)
  starting transfers between devices  25.8 us (9%)
  other arithmetic  18.7 us (6%)
  between operations  13.6 us (5%)
  matrix products  6.15 us (2%)
  local copies, waits for them, and re-layouts  3.37 us (1%)
    psum x1, waiting for transfers between devices, local(): lax.psum((numerator, denominator), ('slab', 'lat'))  94.3 us
    psum x1, blocking collectives, local(): lax.psum((numerator, denominator), ('slab', 'lat'))  40.4 us
    pmax x1, blocking collectives, local(): maximum = lax.pmax(local_max, ('slab', 'lat'))  39.5 us
    ppermute x4, waiting for transfers between devices, with_halo(): lax.ppermute(lax.slice_in_dim(block, 0, width, axis=dim), axis, backward)  24.4 us
    ppermute x4, starting transfers between devices, with_halo(): lax.ppermute(lax.slice_in_dim(block, block.shape[dim] - width, None, axis...  20.5 us
    all_gather x1, waiting for transfers between devices, local(): lax.all_gather(kv_weight, 'lat', axis=2, tiled=True)  13 us
    ppermute x4, waiting for transfers between devices, with_halo(): lax.ppermute(lax.slice_in_dim(block, block.shape[dim] - width, None, axis...  8.15 us
    convert_element_type x1, other arithmetic, local(): hidden = (source + mixed).astype(jnp.bfloat16)  6.96 us
  transfers between devices with their start and end apart: 10, of which 8 were waited for; matrix products, arithmetic and copies ran while one was open for 7% of the time, Pallas kernels for 0%

commit v1 on v0

--- a/solution.py
+++ b/solution.py
@@ -1,7 +1,17 @@
+import functools
 import jax
 import jax.numpy as jnp
 from jax import lax
 from jax.sharding import PartitionSpec as P
+
+
+def move_shifts_all(message, group_axis, across):
+    for pp in (group_axis, across):
+        message = lax.psum(message, pp)
+    return message
+
+
+search_edges_in = functools.partial(move_shifts_all, group_axis="lat", across="slab")
 
 
 def with_halo(block, sides, width):
@@ -67,7 +77,7 @@
     weights_bf = exponent.astype(jnp.bfloat16)
     denominator = jnp.sum(exponent, axis=1)
     numerator = jnp.dot(weights_bf, value_rows, preferred_element_type=jnp.float32)
-    numer_total, denom_total = lax.psum((numerator, denominator), ("slab", "lat"))
+    numer_total, denom_total = search_edges_in((numerator, denominator))
     latents = (numer_total / denom_total[:, None]).astype(jnp.bfloat16)
     back = (
         jnp.einsum("td,ld->tl", token_rows, latents, preferred_element_type=jnp.float32)

time: 289 us -> 304 us (1.052)
  waiting for transfers between devices: 141 us -> 174 us
  blocking collectives: 79.9 us -> 61.6 us
    psum x1 -> x2, waiting for transfers between devices: 94.3 us -> 128 us  [move_shifts_all(): message = lax.psum(message, pp)]
    psum x1 -> x2, blocking collectives: 40.4 us -> 22.1 us  [move_shifts_all(): message = lax.psum(message, pp)]
  transfers between devices with their start and end apart: 10 -> 11, of which waited for: 8 -> 9; matrix products, arithmetic and copies ran while one was open for 7% -> 6% of each run, Pallas kernels for 0% -> 0%
where the time goes in v1:
time: 304 us; the launch traced here: 303 us
  waiting for transfers between devices  174 us (57%)
  blocking collectives  61.6 us (20%)
  starting transfers between devices  25.8 us (8%)
  other arithmetic  18.7 us (6%)
  between operations  13.4 us (4%)
  matrix products  6.15 us (2%)
  local copies, waits for them, and re-layouts  3.37 us (1%)
    psum x2, waiting for transfers between devices, move_shifts_all(): message = lax.psum(message, pp)  128 us
    pmax x1, blocking collectives, local(): maximum = lax.pmax(local_max, ('slab', 'lat'))  39.5 us
    ppermute x4, waiting for transfers between devices, with_halo(): lax.ppermute(lax.slice_in_dim(block, 0, width, axis=dim), axis, backward)  24.4 us
    psum x2, blocking collectives, move_shifts_all(): message = lax.psum(message, pp)  22.1 us
    ppermute x4, starting transfers between devices, with_halo(): lax.ppermute(lax.slice_in_dim(block, block.shape[dim] - width, None, axis...  20.5 us
    all_gather x1, waiting for transfers between devices, local(): lax.all_gather(kv_weight, 'lat', axis=2, tiled=True)  13 us
    ppermute x4, waiting for transfers between devices, with_halo(): lax.ppermute(lax.slice_in_dim(block, block.shape[dim] - width, None, axis...  8.15 us
    convert_element_type x1, other arithmetic, local(): hidden = (source + mixed).astype(jnp.bfloat16)  6.96 us
  transfers between devices with their start and end apart: 11, of which 9 were waited for; matrix products, arithmetic and copies ran while one was open for 6% of the time, Pallas kernels for 0%

profile of v1, /device:TPU:0, one launch (start us, length us, event | category | flops | bytes accessed | tf_op | source)
XLA Modules:
  0.0 303.1 jit_solution(11232818566193787878)
XLA Ops:
  7.3 1.6 fusion.90
  8.9 2.4 collective-permute-start
  11.4 1.3 collective-permute-start.1
  12.7 4.1 %collective-permute-done.1 = bf16[16,4,1,1024]{3,2,1,0:T(2,128)(2,1)S(1)} collective-permute-done((bf16[16,4,1,1024]{3,2,1,0:T(2,128)(2,1)S(1)}, bf16[16,4,1,1024]{3,2,1,0:T(2,128)(2,1)S(1)}, u32[]{:S(2)}, u32[]{:S(2)}) %collective-permute-start.1) | collective-permute-done | bytes 131104 | tf_op jit(solution)/shard_map/ppermute | solution.py:25
  17.3 3.5 %collective-permute-start.2 = (bf16[16,1,4,1024]{3,2,1,0:T(4,128)(2,1)S(1)}, bf16[16,1,4,1024]{3,2,1,0:T(4,128)(2,1)S(1)}, u32[]{:S(2)}, u32[]{:S(2)}) collective-permute-start(bf16[16,1,4,1024]{3,2,1,0:T(4,128)(2,1)S(1)} %get-tuple-element.7), channel_id=1, source_target_pairs={{0,1},{1,2},{2,3},{4,5},{5,6},{6,7},{8,9},{9,10},{10,11},{12,13},{... | collective-permute-start | bytes 393224 | tf_op jit(solution)/shard_map/ppermute | solution.py:22
  22.2 4.1 %collective-permute-done.2 = bf16[16,1,4,1024]{3,2,1,0:T(4,128)(2,1)S(1)} collective-permute-done((bf16[16,1,4,1024]{3,2,1,0:T(4,128)(2,1)S(1)}, bf16[16,1,4,1024]{3,2,1,0:T(4,128)(2,1)S(1)}, u32[]{:S(2)}, u32[]{:S(2)}) %collective-permute-start.2) | collective-permute-done | bytes 131104 | tf_op jit(solution)/shard_map/ppermute | solution.py:22
  26.2 5.3 %collective-permute-done.3 = bf16[16,1,4,1024]{3,2,1,0:T(4,128)(2,1)S(1)} collective-permute-done((bf16[16,1,4,1024]{3,2,1,0:T(4,128)(2,1)S(1)}, bf16[16,1,4,1024]{3,2,1,0:T(4,128)(2,1)S(1)}, u32[]{:S(2)}, u32[]{:S(2)}) %collective-permute-start.3) | collective-permute-done | bytes 131104 | tf_op jit(solution)/shard_map/ppermute | solution.py:25
  32.5 6.8 %fusion.79 = bf16[16,4,2,1024]{3,2,1,0:T(2,128)(2,1)S(1)} fusion(f32[16,6,4,1024]{3,2,1,0:T(4,128)S(1)} %maximum_convert_fusion, f32[1024]{0:T(1024)S(1)} %bitcast.122, f32[1024]{0:T(1024)S(1)} %bitcast.123, f32[1024]{0:T(1024)S(1)} %bitcast.98, f32[1024]{0:T(1024)S(1)} %bitcast.99, f32[1024]{0:T(1024)S(1)} %bitcast.100, f32[1024]{0:T(1024)S(1)} %bitcast.101, ...), kind=kLoop, calls=%fused_computation.126 | loop fusion | flops 8126464 | bytes 6664192 | tf_op jit(solution)/shard_map/convert_element_type | solution.py:54
  39.9 6.2 %collective-permute-start.4 = (bf16[16,4,1,1024]{3,2,1,0:T(2,128)(2,1)S(1)}, bf16[16,4,1,1024]{3,2,1,0:T(2,128)(2,1)S(1)}, u32[]{:S(2)}, u32[]{:S(2)}) collective-permute-start(bf16[16,4,1,1024]{3,2,1,0:T(2,128)(2,1)S(1)} %get-tuple-element.9), channel_id=1, source_target_pairs={{0,4},{4,8},{8,12},{12,16},{16,20},{20,24},{24,28},{1,5},{5,9},{9,... | collective-permute-start | bytes 393224 | tf_op jit(solution)/shard_map/ppermute | solution.py:22
  46.1 1.3 collective-permute-start.5
  47.5 2.7 collective-permute-done.5
  50.7 8.4 %collective-permute-start.6 = (bf16[16,1,4,1024]{3,2,1,0:T(4,128)(2,1)S(1)}, bf16[16,1,4,1024]{3,2,1,0:T(4,128)(2,1)S(1)}, u32[]{:S(2)}, u32[]{:S(2)}) collective-permute-start(bf16[16,1,4,1024]{3,2,1,0:T(4,128)(2,1)S(1)} %get-tuple-element.5), channel_id=1, source_target_pairs={{0,1},{1,2},{2,3},{4,5},{5,6},{6,7},{8,9},{9,10},{10,11},{12,13},{... | collective-permute-start | bytes 393224 | tf_op jit(solution)/shard_map/ppermute | solution.py:22
  60.4 4.1 %collective-permute-done.6 = bf16[16,1,4,1024]{3,2,1,0:T(4,128)(2,1)S(1)} collective-permute-done((bf16[16,1,4,1024]{3,2,1,0:T(4,128)(2,1)S(1)}, bf16[16,1,4,1024]{3,2,1,0:T(4,128)(2,1)S(1)}, u32[]{:S(2)}, u32[]{:S(2)}) %collective-permute-start.6) | collective-permute-done | bytes 131104 | tf_op jit(solution)/shard_map/ppermute | solution.py:22
  64.5 12.2 %collective-permute-done.7 = bf16[16,1,4,1024]{3,2,1,0:T(4,128)(2,1)S(1)} collective-permute-done((bf16[16,1,4,1024]{3,2,1,0:T(4,128)(2,1)S(1)}, bf16[16,1,4,1024]{3,2,1,0:T(4,128)(2,1)S(1)}, u32[]{:S(2)}, u32[]{:S(2)}) %collective-permute-start.7) | collective-permute-done | bytes 131104 | tf_op jit(solution)/shard_map/ppermute | solution.py:25
  77.7 7.0 %fusion.80 = bf16[16,4,2,1024]{3,2,1,0:T(2,128)(2,1)S(1)} fusion(f32[16,6,4,1024]{3,2,1,0:T(4,128)S(1)} %maximum_convert_fusion.1, bf16[16,4,2,1024]{3,2,1,0:T(2,128)(2,1)S(1)} %copy-done.1, f32[1024]{0:T(1024)S(1)} %bitcast.95, f32[1024]{0:T(1024)S(1)} %bitcast.96, f32[1024]{0:T(1024)S(1)} %bitcast.71, f32[1024]{0:T(1024)S(1)} %bitcast.72, ...), kind=kLoop, calls=%fused_computation.127 | loop fusion | flops 8388608 | bytes 6926336 | tf_op jit(solution)/shard_map/convert_element_type | solution.py:59
  84.8 13.0 %all-gather.2.cloned.1.call-done = bf16[2,1024,1024]{2,1,0:T(8,128)(2,1)} async-done(((bf16[2,1024,256]{2,1,0:T(8,128)(2,1)}), bf16[2,1024,1024]{2,1,0:T(8,128)(2,1)}) %all-gather.2.cloned.1.call-update) | async-done | bytes 4194320 | tf_op jit(solution)/shard_map/all_gather | solution.py:64
  97.8 2.9 fusion
  101.2 39.5 %pmax.7 = f32[512]{0:T(512)S(1)} all-reduce(f32[512]{0:T(512)S(1)} %get-tuple-element.67), channel_id=1, replica_groups=mesh['slab'=8,'lat'=4] {'slab','lat'}, use_global_device_ids=true, to_apply=%region_1.2 | all-reduce | flops 512 | bytes 4096 | tf_op jit(solution)/shard_map/pmax | solution.py:75
  140.7 1.8 fusion.81
  142.5 86.0 %all-reduce.5.cloned.1.call-done = f32[512,1024]{1,0:T(8,128)} async-done(((f32[512,1024]{1,0:T(8,128)}), f32[512,1024]{1,0:T(8,128)}) %all-reduce.5.cloned.1.call-update) | async-done | bytes 2097168 | tf_op jit(solution)/shard_map/psum | solution.py:10
  228.7 10.0 %psum.30 = f32[512]{0:T(512)S(1)} all-reduce(f32[512]{0:T(512)S(1)} %fusion.82), channel_id=1, replica_groups=mesh['slab'=8,'lat'=4] {'lat'}, use_global_device_ids=true, to_apply=%region_5.6 | all-reduce | flops 512 | bytes 4096 | tf_op jit(solution)/shard_map/psum | solution.py:10
  238.7 12.1 %psum.31 = f32[512]{0:T(512)S(1)} all-reduce(f32[512]{0:T(512)S(1)} %psum.30), channel_id=1, replica_groups=mesh['slab'=8,'lat'=4] {'slab'}, use_global_device_ids=true, to_apply=%region_6.7 | all-reduce | flops 512 | bytes 4096 | tf_op jit(solution)/shard_map/psum | solution.py:10
  250.8 41.9 %all-reduce.7.cloned.1.call-done = f32[512,1024]{1,0:T(8,128)} async-done(((f32[512,1024]{1,0:T(8,128)}), f32[512,1024]{1,0:T(8,128)}) %all-reduce.7.cloned.1.call-update) | async-done | bytes 2097168 | tf_op jit(solution)/shard_map/psum | solution.py:10
  292.7 1.9 divide_convert_fusion
  (35 shorter events, 9.7 us)
Async XLA Ops:
  6.5 94.1 %copy-start = (bf16[512,1024]{1,0:T(8,128)(2,1)S(1)}, bf16[512,1024]{1,0:T(8,128)(2,1)}, u32[]{:S(2)}) copy-start(bf16[512,1024]{1,0:T(8,128)(2,1)} %param.9) | copy-start | bytes 3145732
  6.5 10.3 %copy-start.1 = (bf16[16,4,2,1024]{3,2,1,0:T(2,128)(2,1)S(1)}, bf16[16,4,2,1024]{3,2,1,0:T(2,128)(2,1)}, u32[]{:S(2)}) copy-start(bf16[16,4,2,1024]{3,2,1,0:T(2,128)(2,1)} %param.5) | copy-start | bytes 786436
  6.5 6.1 %copy-start.2 = (f32[27,1024]{1,0:T(8,128)S(1)}, f32[27,1024]{1,0:T(8,128)}, u32[]{:S(2)}) copy-start(f32[27,1024]{1,0:T(8,128)} %param.6) | copy-start | bytes 331780
  6.5 91.2 %all-gather.2.cloned.1.call-start = ((), (), s32[]{:S(2)}) async-start(), calls=%async_computation | async-start | bytes 5242880 | tf_op jit(solution)/shard_map/all_gather | solution.py:64
  7.3 221.3 %all-reduce.5.cloned.1.call-start = ((), (), s32[]{:S(2)}) async-start(), calls=%async_computation.1 | async-start | bytes 4194304 | tf_op jit(solution)/shard_map/psum | solution.py:10
  8.9 3.8 %collective-permute-start = (bf16[16,4,1,1024]{3,2,1,0:T(2,128)(2,1)S(1)}, bf16[16,4,1,1024]{3,2,1,0:T(2,128)(2,1)S(1)}, u32[]{:S(2)}, u32[]{:S(2)}) collective-permute-start(bf16[16,4,1,1024]{3,2,1,0:T(2,128)(2,1)S(1)} %get-tuple-element.11), channel_id=1, source_target_pairs={{0,4},{4,8},{8,12},{12,16},{16,20},{20,24},{24,28},{1,5},{5,9},{9,... | collective-permute-start | bytes 393224 | tf_op jit(solution)/shard_map/ppermute | solution.py:22
  11.4 5.5 %collective-permute-start.1 = (bf16[16,4,1,1024]{3,2,1,0:T(2,128)(2,1)S(1)}, bf16[16,4,1,1024]{3,2,1,0:T(2,128)(2,1)S(1)}, u32[]{:S(2)}, u32[]{:S(2)}) collective-permute-start(bf16[16,4,1,1024]{3,2,1,0:T(2,128)(2,1)S(1)} %get-tuple-element.12), channel_id=1, source_target_pairs={{4,0},{8,4},{12,8},{16,12},{20,16},{24,20},{28,24},{5,1},{9,5},{13... | collective-permute-start | bytes 393224 | tf_op jit(solution)/shard_map/ppermute | solution.py:25
  17.3 8.9 %collective-permute-start.2 = (bf16[16,1,4,1024]{3,2,1,0:T(4,128)(2,1)S(1)}, bf16[16,1,4,1024]{3,2,1,0:T(4,128)(2,1)S(1)}, u32[]{:S(2)}, u32[]{:S(2)}) collective-permute-start(bf16[16,1,4,1024]{3,2,1,0:T(4,128)(2,1)S(1)} %get-tuple-element.7), channel_id=1, source_target_pairs={{0,1},{1,2},{2,3},{4,5},{5,6},{6,7},{8,9},{9,10},{10,11},{12,13},{... | collective-permute-start | bytes 393224 | tf_op jit(solution)/shard_map/ppermute | solution.py:22
  20.8 10.7 %collective-permute-start.3 = (bf16[16,1,4,1024]{3,2,1,0:T(4,128)(2,1)S(1)}, bf16[16,1,4,1024]{3,2,1,0:T(4,128)(2,1)S(1)}, u32[]{:S(2)}, u32[]{:S(2)}) collective-permute-start(bf16[16,1,4,1024]{3,2,1,0:T(4,128)(2,1)S(1)} %get-tuple-element.8), channel_id=1, source_target_pairs={{1,0},{2,1},{3,2},{5,4},{6,5},{7,6},{9,8},{10,9},{11,10},{13,12},{... | collective-permute-start | bytes 393224 | tf_op jit(solution)/shard_map/ppermute | solution.py:25
  32.5 14.9 %copy-start.3 = (f32[27,1024]{1,0:T(8,128)S(1)}, f32[27,1024]{1,0:T(8,128)}, u32[]{:S(2)}) copy-start(f32[27,1024]{1,0:T(8,128)} %param.7) | copy-start | bytes 331780
  39.9 7.6 %collective-permute-start.4 = (bf16[16,4,1,1024]{3,2,1,0:T(2,128)(2,1)S(1)}, bf16[16,4,1,1024]{3,2,1,0:T(2,128)(2,1)S(1)}, u32[]{:S(2)}, u32[]{:S(2)}) collective-permute-start(bf16[16,4,1,1024]{3,2,1,0:T(2,128)(2,1)S(1)} %get-tuple-element.9), channel_id=1, source_target_pairs={{0,4},{4,8},{8,12},{12,16},{16,20},{20,24},{24,28},{1,5},{5,9},{9,... | collective-permute-start | bytes 393224 | tf_op jit(solution)/shard_map/ppermute | solution.py:22
  46.1 4.1 %collective-permute-start.5 = (bf16[16,4,1,1024]{3,2,1,0:T(2,128)(2,1)S(1)}, bf16[16,4,1,1024]{3,2,1,0:T(2,128)(2,1)S(1)}, u32[]{:S(2)}, u32[]{:S(2)}) collective-permute-start(bf16[16,4,1,1024]{3,2,1,0:T(2,128)(2,1)S(1)} %get-tuple-element.10), channel_id=1, source_target_pairs={{4,0},{8,4},{12,8},{16,12},{20,16},{24,20},{28,24},{5,1},{9,5},{13... | collective-permute-start | bytes 393224 | tf_op jit(solution)/shard_map/ppermute | solution.py:25
  50.7 13.8 %collective-permute-start.6 = (bf16[16,1,4,1024]{3,2,1,0:T(4,128)(2,1)S(1)}, bf16[16,1,4,1024]{3,2,1,0:T(4,128)(2,1)S(1)}, u32[]{:S(2)}, u32[]{:S(2)}) collective-permute-start(bf16[16,1,4,1024]{3,2,1,0:T(4,128)(2,1)S(1)} %get-tuple-element.5), channel_id=1, source_target_pairs={{0,1},{1,2},{2,3},{4,5},{5,6},{6,7},{8,9},{9,10},{10,11},{12,13},{... | collective-permute-start | bytes 393224 | tf_op jit(solution)/shard_map/ppermute | solution.py:22
  59.1 17.6 %collective-permute-start.7 = (bf16[16,1,4,1024]{3,2,1,0:T(4,128)(2,1)S(1)}, bf16[16,1,4,1024]{3,2,1,0:T(4,128)(2,1)S(1)}, u32[]{:S(2)}, u32[]{:S(2)}) collective-permute-start(bf16[16,1,4,1024]{3,2,1,0:T(4,128)(2,1)S(1)} %get-tuple-element.6), channel_id=1, source_target_pairs={{1,0},{2,1},{3,2},{5,4},{6,5},{7,6},{9,8},{10,9},{11,10},{13,12},{... | collective-permute-start | bytes 393224 | tf_op jit(solution)/shard_map/ppermute | solution.py:25
  142.5 150.2 %all-reduce.7.cloned.1.call-start = ((), (), s32[]{:S(2)}) async-start(), calls=%async_computation.2 | async-start | bytes 4194304 | tf_op jit(solution)/shard_map/psum | solution.py:10
Sparse Core Ops, SparseCore 0:
  8.9 88.8 all-gather.1
  142.6 85.8 all-reduce.4
  231.8 60.8 all-reduce.6
